TPU v7x, 256 devices: a whole 4x4x8 slice. The times are simulated.
256 devices in a mesh: visit: 32 (over z_lo, y, core), tile: 8 (over z_hi, x).
Axes of the slice: x: 4, y: 4, z: 8 (z_hi: 2, z_lo: 4; z = z_hi * 4 + z_lo), core: 2. Of those that a mesh axis runs over, the one named last changes fastest.
Arguments:
- exposures: float32 [32, 2048, 256], P('visit', 'tile'), may hold values from 0.3 to 3
- sky_model: float32 [2048, 256], P(('tile', 'visit')), may hold values from 0.5 to 2
- blur_kernels: float32 [32, 31, 31], P('visit'), may hold values from 0.05 to 1
- coverage: int32 [32, 8], P('visit'), may hold values from 0 to 1, as said below
Outputs:
- deconvolved: float32 [2048, 256], P(('tile', 'visit'))
Inputs may be any that keep to these rules, and one draw needn't show every extreme that they name: `coverage`: every tile is covered by at least one exposure.
All inputs are finite; a program needn't handle non-finite values.
Results may differ from a plain program's by a relative error of at most 0.0001.
Values sent between devices are 32-bit elements; how exact they have to be, the bound alone decides.
A program may use at most 128 MiB of HBM per device.

v0:
```python
import jax
import jax.numpy as jnp
from jax import lax
from jax.sharding import PartitionSpec as P

ITERS = 2


def padded(array, sides, width):
    for axis, dim in sides:
        peers, length = (lax.axis_size(axis), array.shape[dim])
        up = [(i, (i + 1) % peers) for i in range(peers - 1)]
        down = [(j, i) for i, j in up]
        last = lax.slice_in_dim(array, length - width, length, axis=dim)
        initial = lax.slice_in_dim(array, 0, width, axis=dim)
        before = lax.ppermute(last, axis, up)
        after = lax.ppermute(initial, axis, down)
        array = jnp.concatenate([before, array, after], axis=dim)
    return array


def band_lookup(width, kernel_len):
    half = kernel_len // 2
    differ = jnp.arange(width)[:, None] - jnp.arange(width)[None, :] + half
    band_table = (differ[:, :, None] == jnp.arange(kernel_len)[None, None, :]).astype(jnp.float32)
    return band_table.reshape(width * width, kernel_len)


def column_operator(kernel, band_table, width):
    kernel_len = kernel.shape[0]
    operator = jnp.dot(band_table, kernel.T, precision=lax.Precision.HIGHEST)
    operator = operator.reshape(width, width, kernel_len).transpose(0, 2, 1)
    return operator.reshape(width, kernel_len * width)


def correlate(extended, operator):
    width = operator.shape[0]
    kernel_len = operator.shape[1] // width
    out_rows = extended.shape[0] - (kernel_len - 1)
    product = jnp.dot(extended, operator, precision=lax.Precision.HIGHEST)
    product = product.reshape(extended.shape[0], kernel_len, width)
    total = product[0:out_rows, 0]
    for offset in range(1, kernel_len):
        total = total + product[offset : offset + out_rows, offset]
    return total


def body(exposures, sky_model, blur_kernels, coverage):
    tile_rows = exposures.shape[1]
    tile_cols = exposures.shape[2]
    kernel_len = blur_kernels.shape[1]
    radius = kernel_len // 2
    tile_count = lax.axis_size("tile")
    tile_place = lax.axis_index("tile")
    kernels = blur_kernels / jnp.sum(blur_kernels, axis=(1, 2), keepdims=True)
    band_table = band_lookup(tile_cols, kernel_len)
    forward_ops = [column_operator(kernels[0], band_table, tile_cols)]
    flipped_ops = [column_operator(kernels[0][::-1, ::-1], band_table, tile_cols)]
    global_row = tile_place * tile_rows - radius + jnp.arange(tile_rows + 2 * radius)
    row_owner = jnp.floor_divide(global_row, tile_rows)
    selector = (row_owner[:, None] == jnp.arange(tile_count)[None, :]).astype(jnp.float32)
    weight_rows = jnp.dot(coverage.astype(jnp.float32), selector.T, precision=lax.Precision.HIGHEST)
    own_weights = weight_rows[:, radius : radius + tile_rows]
    member = 0
    column_sums = forward_ops[member].reshape(tile_cols, kernel_len, tile_cols).sum(axis=0)
    row_window = jnp.stack(
        [weight_rows[member][offset : offset + tile_rows] for offset in range(kernel_len)], axis=1
    )
    norm_local = jnp.dot(row_window, column_sums, precision=lax.Precision.HIGHEST)
    norm_shard = lax.psum_scatter(norm_local, "visit", scatter_dimension=0, tiled=True)
    model_shard = sky_model
    for step in range(ITERS):
        whole = lax.all_gather(model_shard, "visit", axis=0, tiled=True)
        model_wide = padded(whole, (("tile", 0),), radius)
        member = 0
        blurred = correlate(model_wide, flipped_ops[member])
        ratio_list = [own_weights[member][:, None] * exposures[member] / blurred]
        ratios = jnp.stack(ratio_list)
        ratio_wide = padded(ratios, (("tile", 1),), radius)
        member = 0
        numerator = correlate(ratio_wide[member], forward_ops[member])
        update = lax.psum_scatter(numerator, "visit", scatter_dimension=0, tiled=True)
        model_shard = model_shard * update / norm_shard
    return model_shard


def solution(mesh):
    return jax.shard_map(
        body,
        mesh=mesh,
        in_specs=(
            P("visit", "tile", None),
            P(("tile", "visit"), None),
            P("visit", None, None),
            P("visit", None),
        ),
        out_specs=P(("tile", "visit"), None),
        check_vma=False,
    )
```

profile of v0, /device:TPU:2, one launch (start us, length us, event | category | flops | bytes accessed | tf_op | source)
XLA Modules:
  0.0 643.0 jit_solution(17559654957804409515)
XLA Ops:
  6.5 45.5 %all_gather.6 = f32[256,256]{1,0:T(8,128)S(1)} all-gather(f32[8,256]{1,0:T(8,128)} %param.5), channel_id=1, replica_groups=mesh['visit'=32,'tile'=8] {'visit'}, dimensions={0}, use_global_device_ids=true | all-gather | bytes 270336 | tf_op jit(solution)/shard_map/all_gather | solution.py:73
  52.1 3.4 collective-permute-start
  55.5 2.4 collective-permute-start.1
  58.0 1.4 reduce_sum.18
  59.3 1.4 broadcast_divide_fusion
  60.7 0.1 rev.3
  60.8 0.9 fusion.116
  61.8 0.1 fusion.114
  61.8 6.3 fusion.117
  68.2 6.1 fusion.17
  74.2 0.1 fusion.115
  74.3 0.1 slice.660
  74.4 10.0 %copy.7 = f32[256,31,256]{0,2,1:T(8,128)} copy(f32[256,31,256]{2,1,0:T(8,128)} %fusion.17) | data formatting | bytes 16252928 | tf_op jit(solution)/shard_map/transpose | solution.py:32
  84.3 0.1 stack.129
  84.5 0.0 collective-permute-done
  84.5 0.0 collective-permute-done.1
  84.5 11.2 %fusion.10 = f32[286,31,256]{2,0,1:T(8,128)S(1)} fusion(f32[256,31,256]{0,2,1:T(8,128)} %copy.7, f32[15,256]{1,0:T(8,128)S(1)} %collective-permute-done.1, f32[256,256]{1,0:T(8,128)S(1)} %all_gather.6, f32[15,256]{1,0:T(8,128)S(1)} %collective-permute-done), kind=kOutput, calls=%fused_computation.11 | convolution fusion | flops 6972652544 | bytes 17498112 | tf_op jit(solution)/shard_map/dot_general | solution.py:40
  95.7 0.8 fusion.81
  96.5 3.4 collective-permute-start.2
  99.9 2.4 collective-permute-start.3
  102.4 1.1 fusion.118
  103.5 0.0 reduce-scatter.6.cloned.1.call-update
  103.5 0.2 reduce-scatter.4.cloned.1.call-start
  103.8 9.9 %copy.8 = f32[256,31,256]{0,2,1:T(8,128)} copy(f32[256,31,256]{2,1,0:T(8,128)} %get-tuple-element.47) | data formatting | bytes 16252928 | tf_op jit(solution)/shard_map/transpose | solution.py:32
  113.7 0.0 collective-permute-done.2
  113.7 0.0 collective-permute-done.3
  113.7 11.2 %fusion.6 = f32[286,31,256]{2,0,1:T(8,128)S(1)} fusion(f32[256,31,256]{0,2,1:T(8,128)} %copy.8, f32[1,15,256]{2,1,0:T(8,128)S(1)} %collective-permute-done.3, f32[1,256,256]{2,1,0:T(8,128)S(1)} %fusion.81, f32[1,15,256]{2,1,0:T(8,128)S(1)} %collective-permute-done.2), kind=kOutput, calls=%fused_computation.7 | convolution fusion | flops 6972652544 | bytes 17498112 | tf_op jit(solution)/shard_map/dot_general | solution.py:40
  124.9 0.0 copy-start.1
  124.9 1.4 fusion.65
  126.3 0.0 reduce-scatter.4.cloned.1.call-update
  126.3 0.0 reduce-scatter.8.cloned.1.call-start
  126.4 130.0 %reduce-scatter.6.cloned.1.call-done = f32[8,256]{1,0:T(8,128)} async-done(((f32[256,256]{1,0:T(8,128)}), f32[8,256]{1,0:T(8,128)}) %reduce-scatter.6.cloned.1.call-update) | async-done | bytes 8208 | tf_op jit(solution)/shard_map/reduce_scatter | solution.py:70
  256.4 144.5 %reduce-scatter.4.cloned.1.call-done = f32[8,256]{1,0:T(8,128)} async-done(((f32[256,256]{1,0:T(8,128)}), f32[8,256]{1,0:T(8,128)}) %reduce-scatter.4.cloned.1.call-update) | async-done | bytes 8208 | tf_op jit(solution)/shard_map/reduce_scatter | solution.py:82
  400.9 0.7 multiply_divide_fusion.1
  401.6 38.3 %all_gather.7 = f32[256,256]{1,0:T(8,128)S(1)} all-gather(f32[8,256]{1,0:T(8,128)S(1)} %multiply_divide_fusion.1), channel_id=1, replica_groups=mesh['visit'=32,'tile'=8] {'visit'}, dimensions={0}, use_global_device_ids=true | all-gather | bytes 270336 | tf_op jit(solution)/shard_map/all_gather | solution.py:73
  439.9 3.8 collective-permute-start.4
  443.7 2.0 collective-permute-start.5
  445.7 3.6 collective-permute-done.5
  449.3 11.2 %fusion.8 = f32[286,31,256]{2,0,1:T(8,128)S(1)} fusion(f32[256,31,256]{0,2,1:T(8,128)} %copy.7, f32[15,256]{1,0:T(8,128)S(1)} %collective-permute-done.5, f32[256,256]{1,0:T(8,128)S(1)} %all_gather.7, f32[15,256]{1,0:T(8,128)S(1)} %collective-permute-done.4), kind=kOutput, calls=%fused_computation.9 | convolution fusion | flops 6972652544 | bytes 17498112 | tf_op jit(solution)/shard_map/dot_general | solution.py:40
  460.5 0.8 fusion.50
  461.3 3.7 collective-permute-start.6
  465.0 2.4 collective-permute-start.7
  467.4 9.2 %collective-permute-done.7 = f32[1,15,256]{2,1,0:T(8,128)S(1)} collective-permute-done((f32[1,15,256]{2,1,0:T(8,128)S(1)}, f32[1,15,256]{2,1,0:T(8,128)S(1)}, u32[]{:S(2)}, u32[]{:S(2)}) %collective-permute-start.7) | collective-permute-done | bytes 15392 | tf_op jit(solution)/shard_map/ppermute | solution.py:17
  476.6 11.2 %fusion.4 = f32[286,31,256]{2,0,1:T(8,128)S(1)} fusion(f32[256,31,256]{0,2,1:T(8,128)} %copy.8, f32[1,15,256]{2,1,0:T(8,128)S(1)} %collective-permute-done.7, f32[1,256,256]{2,1,0:T(8,128)S(1)} %fusion.50, f32[1,15,256]{2,1,0:T(8,128)S(1)} %collective-permute-done.6), kind=kOutput, calls=%fused_computation.5 | convolution fusion | flops 6972652544 | bytes 17498112 | tf_op jit(solution)/shard_map/dot_general | solution.py:40
  487.8 1.4 fusion.34
  489.3 0.0 reduce-scatter.8.cloned.1.call-update
  489.3 145.9 %reduce-scatter.8.cloned.1.call-done = f32[8,256]{1,0:T(8,128)} async-done(((f32[256,256]{1,0:T(8,128)}), f32[8,256]{1,0:T(8,128)}) %reduce-scatter.8.cloned.1.call-update) | async-done | bytes 8208 | tf_op jit(solution)/shard_map/reduce_scatter | solution.py:82
  635.2 1.3 multiply_divide_fusion
  (15 shorter events, 0.1 us)
Async XLA Ops:
  6.5 249.8 %reduce-scatter.6.cloned.1.call-start = ((), (), s32[]{:S(2)}) async-start(), calls=%async_computation.4 | async-start | bytes 270336 | tf_op jit(solution)/shard_map/reduce_scatter | solution.py:70
  52.1 32.4 %collective-permute-start = (f32[15,256]{1,0:T(8,128)S(1)}, f32[15,256]{1,0:T(8,128)S(1)}, u32[]{:S(2)}, u32[]{:S(2)}) collective-permute-start(f32[15,256]{1,0:T(8,128)S(1)} %get-tuple-element.11), channel_id=1, source_target_pairs={{0,1},{1,2},{2,3},{3,4},{4,5},{5,6},{6,7},{8,9},{9,10},{10,11},{11... | collective-permute-start | bytes 46088 | tf_op jit(solution)/shard_map/ppermute | solution.py:16
  55.5 29.0 %collective-permute-start.1 = (f32[15,256]{1,0:T(8,128)S(1)}, f32[15,256]{1,0:T(8,128)S(1)}, u32[]{:S(2)}, u32[]{:S(2)}) collective-permute-start(f32[15,256]{1,0:T(8,128)S(1)} %get-tuple-element.12), channel_id=1, source_target_pairs={{1,0},{2,1},{3,2},{4,3},{5,4},{6,5},{7,6},{9,8},{10,9},{11,10},{12... | collective-permute-start | bytes 46088 | tf_op jit(solution)/shard_map/ppermute | solution.py:17
  84.4 11.3 %copy-start = (f32[1,256,256]{2,1,0:T(8,128)S(1)}, f32[1,256,256]{2,1,0:T(8,128)}, u32[]{:S(2)}) copy-start(f32[1,256,256]{2,1,0:T(8,128)} %param.4) | copy-start | bytes 786436
  96.5 17.1 %collective-permute-start.2 = (f32[1,15,256]{2,1,0:T(8,128)S(1)}, f32[1,15,256]{2,1,0:T(8,128)S(1)}, u32[]{:S(2)}, u32[]{:S(2)}) collective-permute-start(f32[1,15,256]{2,1,0:T(8,128)S(1)} %get-tuple-element.9), channel_id=1, source_target_pairs={{0,1},{1,2},{2,3},{3,4},{4,5},{5,6},{6,7},{8,9},{9,10},{10,11},{11... | collective-permute-start | bytes 46088 | tf_op jit(solution)/shard_map/ppermute | solution.py:16
  99.9 13.7 %collective-permute-start.3 = (f32[1,15,256]{2,1,0:T(8,128)S(1)}, f32[1,15,256]{2,1,0:T(8,128)S(1)}, u32[]{:S(2)}, u32[]{:S(2)}) collective-permute-start(f32[1,15,256]{2,1,0:T(8,128)S(1)} %get-tuple-element.10), channel_id=1, source_target_pairs={{1,0},{2,1},{3,2},{4,3},{5,4},{6,5},{7,6},{9,8},{10,9},{11,10},{12... | collective-permute-start | bytes 46088 | tf_op jit(solution)/shard_map/ppermute | solution.py:17
  103.5 297.4 %reduce-scatter.4.cloned.1.call-start = ((), (), s32[]{:S(2)}) async-start(), calls=%async_computation.3 | async-start | bytes 270336 | tf_op jit(solution)/shard_map/reduce_scatter | solution.py:82
  124.9 276.0 %copy-start.1 = (f32[8,256]{1,0:T(8,128)S(1)}, f32[8,256]{1,0:T(8,128)}, u32[]{:S(2)}) copy-start(f32[8,256]{1,0:T(8,128)} %param.5) | copy-start | bytes 24580
  126.3 508.8 %reduce-scatter.8.cloned.1.call-start = ((), (), s32[]{:S(2)}) async-start(), calls=%async_computation.5 | async-start | bytes 270336 | tf_op jit(solution)/shard_map/reduce_scatter | solution.py:82
  439.9 5.8 collective-permute-start.4
  443.7 5.6 collective-permute-start.5
  461.3 6.1 collective-permute-start.6
  465.0 11.6 %collective-permute-start.7 = (f32[1,15,256]{2,1,0:T(8,128)S(1)}, f32[1,15,256]{2,1,0:T(8,128)S(1)}, u32[]{:S(2)}, u32[]{:S(2)}) collective-permute-start(f32[1,15,256]{2,1,0:T(8,128)S(1)} %get-tuple-element.6), channel_id=1, source_target_pairs={{1,0},{2,1},{3,2},{4,3},{5,4},{6,5},{7,6},{9,8},{10,9},{11,10},{12... | collective-permute-start | bytes 46088 | tf_op jit(solution)/shard_map/ppermute | solution.py:17
  487.8 147.3 %copy-start.2 = (f32[8,256]{1,0:T(8,128)S(1)}, f32[8,256]{1,0:T(8,128)}, u32[]{:S(2)}) copy-start(f32[8,256]{1,0:T(8,128)} %reduce-scatter.6.cloned.1.call-done) | copy-start | bytes 24580
Sparse Core Ops, SparseCore 0:
  103.7 152.6 reduce-scatter.5
  258.9 141.9 reduce-scatter.3
  489.4 145.6 reduce-scatter.7
where the time goes:
time: 644 us; the launch traced here: 643 us
  waiting for transfers between devices  433 us (67%)
  blocking collectives  83.8 us (13%)
  matrix products  59.2 us (9%)
  starting transfers between devices  23.8 us (4%)
  local copies, waits for them, and re-layouts  20.3 us (3%)
  between operations  13.3 us (2%)
  other arithmetic  9.28 us (1%)
    reduce_scatter x2, waiting for transfers between devices, body(): lax.psum_scatter(numerator, 'visit', scatter_dimension=0, tiled=True)  290 us
    reduce_scatter x1, waiting for transfers between devices, body(): lax.psum_scatter(norm_local, 'visit', scatter_dimension=0, tiled=True)  130 us
    all_gather x2, blocking collectives, body(): whole = lax.all_gather(model_shard, 'visit', axis=0, tiled=True)  83.8 us
    dot_general x4, matrix products, correlate(): product = jnp.dot(extended, operator, precision=lax.Precision.HIGHEST)  44.8 us
    transpose x2, local copies, waits for them, and re-layouts, column_operator(): operator = operator.reshape(width, width, kernel_len).transpose(0, 2, 1)  19.9 us
    ppermute x4, starting transfers between devices, padded(): before = lax.ppermute(last, axis, up)  14.3 us
  transfers between devices with their start and end apart: 11, of which 5 were waited for; matrix products, arithmetic and copies ran while one was open for 8% of the time, Pallas kernels for 0%

commit v1 on v0

--- a/solution.py
+++ b/solution.py
@@ -70,7 +70,9 @@
     norm_shard = lax.psum_scatter(norm_local, "visit", scatter_dimension=0, tiled=True)
     model_shard = sky_model
     for step in range(ITERS):
-        whole = lax.all_gather(model_shard, "visit", axis=0, tiled=True)
+        whole = jnp.concatenate(
+            lax.all_to_all(jnp.stack([model_shard] * lax.axis_size("visit")), "visit", 0, 0), axis=0
+        )
         model_wide = padded(whole, (("tile", 0),), radius)
         member = 0
         blurred = correlate(model_wide, flipped_ops[member])

time: 644 us -> 587 us (0.911)
  blocking collectives: 83.8 us -> 14.3 us
  starting transfers between devices: 23.8 us -> 34.6 us
    all_gather x2 -> x0, blocking collectives: 83.8 us -> none  [body(): whole = lax.all_gather(model_shard, 'visit', axis=0, tiled=True)]
    all_to_all x0 -> x1, blocking collectives: none -> 14.3 us  [body(): lax.all_to_all(jnp.stack([model_shard] * lax.axis_size('visit')), 'visit'...]
    all_to_all x0 -> x1, starting transfers between devices: none -> 8.92 us  [body(): lax.all_to_all(jnp.stack([model_shard] * lax.axis_size('visit')), 'visit'...]
  transfers between devices with their start and end apart: 11 -> 12, of which waited for: 5 -> 5; matrix products, arithmetic and copies ran while one was open for 8% -> 9% of each run, Pallas kernels for 0% -> 0%
where the time goes in v1:
time: 587 us; the launch traced here: 586 us
  waiting for transfers between devices  436 us (74%)
  matrix products  57 us (10%)
  starting transfers between devices  34.6 us (6%)
  local copies, waits for them, and re-layouts  21.7 us (4%)
  blocking collectives  14.3 us (2%)
  between operations  13.4 us (2%)
  other arithmetic  9.25 us (2%)
    reduce_scatter x2, waiting for transfers between devices, body(): lax.psum_scatter(numerator, 'visit', scatter_dimension=0, tiled=True)  290 us
    reduce_scatter x1, waiting for transfers between devices, body(): lax.psum_scatter(norm_local, 'visit', scatter_dimension=0, tiled=True)  133 us
    dot_general x4, matrix products, correlate(): product = jnp.dot(extended, operator, precision=lax.Precision.HIGHEST)  42.5 us
    transpose x2, local copies, waits for them, and re-layouts, column_operator(): operator = operator.reshape(width, width, kernel_len).transpose(0, 2, 1)  19.8 us
    ppermute x4, starting transfers between devices, padded(): before = lax.ppermute(last, axis, up)  15.6 us
    all_to_all x1, blocking collectives, body(): lax.all_to_all(jnp.stack([model_shard] * lax.axis_size('visit')), 'visit'...  14.3 us
    ppermute x4, waiting for transfers between devices, padded(): after = lax.ppermute(initial, axis, down)  12.7 us
    dot_general x2, matrix products, column_operator(): operator = jnp.dot(band_table, kernel.T, precision=lax.Precision.HIGHEST)  12.4 us
  transfers between devices with their start and end apart: 12, of which 5 were waited for; matrix products, arithmetic and copies ran while one was open for 9% of the time, Pallas kernels for 0%

profile of v1, /device:TPU:2, one launch (start us, length us, event | category | flops | bytes accessed | tf_op | source)
XLA Modules:
  0.0 586.4 jit_solution(15270421899262981177)
XLA Ops:
  6.5 1.4 stack.68
  7.9 8.9 %all-to-all-start = ((f32[32,8,256]{2,1,0:T(8,128)}), f32[32,8,256]{2,1,0:T(8,128)S(1)}, u32[]{:S(2)}, u32[]{:S(2)}) async-start(f32[32,8,256]{2,1,0:T(8,128)} %stack.68), calls=%async_computation | async-start | bytes 524288 | tf_op jit(solution)/shard_map/all_to_all | solution.py:74
  16.9 0.0 reduce-scatter.6.cloned.1.call-start
  17.0 1.4 reduce_sum.18
  18.3 1.4 broadcast_divide_fusion
  19.7 0.9 fusion.116
  20.6 6.3 %fusion.117 = (f32[31,256]{1,0:T(8,128)S(1)}, f32[256,31,256]{2,1,0:T(8,128)}) fusion(f32[1,31,31]{2,0,1:T(1,128)S(1)} %broadcast_divide_fusion, s32[256,256]{1,0:T(8,128)S(1)} %subtract_add_fusion), kind=kOutput, calls=%fused_computation.252 | convolution fusion | flops 759816448 | bytes 8424196 | tf_op jit(solution)/shard_map/dot_general | solution.py:31
  27.0 0.1 fusion.114
  27.1 0.1 rev.3
  27.1 6.1 %fusion.17 = f32[256,31,256]{2,1,0:T(8,128)} fusion(s32[256,256]{1,0:T(8,128)S(1)} %subtract_add_fusion, f32[31,31]{1,0:T(8,128)S(1)} %rev.3), kind=kOutput, calls=%fused_computation.16 | convolution fusion | flops 757792768 | bytes 8392452 | tf_op jit(solution)/shard_map/dot_general | solution.py:31
  33.3 3.4 collective-permute-start
  36.7 2.4 collective-permute-start.1
  39.1 0.1 fusion.115
  39.2 0.1 slice.660
  39.3 9.9 %copy.7 = f32[256,31,256]{0,2,1:T(8,128)} copy(f32[256,31,256]{2,1,0:T(8,128)} %fusion.17) | data formatting | bytes 16252928 | tf_op jit(solution)/shard_map/transpose | solution.py:32
  49.2 0.1 stack.200
  49.3 0.0 collective-permute-done.1
  49.3 11.2 %fusion.10 = f32[286,31,256]{2,0,1:T(8,128)S(1)} fusion(f32[256,31,256]{0,2,1:T(8,128)} %copy.7, f32[15,256]{1,0:T(8,128)S(1)} %collective-permute-done.1, f32[256,256]{1,0:T(8,128)S(1)} %bitcast.447, f32[15,256]{1,0:T(8,128)S(1)} %collective-permute-done), kind=kOutput, calls=%fused_computation.11 | convolution fusion | flops 6972652544 | bytes 17498112 | tf_op jit(solution)/shard_map/dot_general | solution.py:40
  60.6 0.8 fusion.81
  61.4 3.4 collective-permute-start.2
  64.8 2.4 collective-permute-start.3
  67.2 1.1 fusion.118
  68.4 0.0 reduce-scatter.6.cloned.1.call-update
  68.4 0.2 reduce-scatter.4.cloned.1.call-start
  68.6 9.9 %copy.8 = f32[256,31,256]{0,2,1:T(8,128)} copy(f32[256,31,256]{2,1,0:T(8,128)} %get-tuple-element.47) | data formatting | bytes 16252928 | tf_op jit(solution)/shard_map/transpose | solution.py:32
  78.5 0.0 collective-permute-done.2
  78.5 11.2 %fusion.6 = f32[286,31,256]{2,0,1:T(8,128)S(1)} fusion(f32[256,31,256]{0,2,1:T(8,128)} %copy.8, f32[1,15,256]{2,1,0:T(8,128)S(1)} %collective-permute-done.3, f32[1,256,256]{2,1,0:T(8,128)S(1)} %fusion.81, f32[1,15,256]{2,1,0:T(8,128)S(1)} %collective-permute-done.2), kind=kOutput, calls=%fused_computation.7 | convolution fusion | flops 6972652544 | bytes 17498112 | tf_op jit(solution)/shard_map/dot_general | solution.py:40
  89.7 0.0 copy-start.1
  89.7 1.4 fusion.65
  91.2 0.0 reduce-scatter.4.cloned.1.call-update
  91.2 0.0 reduce-scatter.8.cloned.1.call-start
  91.2 133.2 %reduce-scatter.6.cloned.1.call-done = f32[8,256]{1,0:T(8,128)} async-done(((f32[256,256]{1,0:T(8,128)}), f32[8,256]{1,0:T(8,128)}) %reduce-scatter.6.cloned.1.call-update) | async-done | bytes 8208 | tf_op jit(solution)/shard_map/reduce_scatter | solution.py:70
  224.4 144.2 %reduce-scatter.4.cloned.1.call-done = f32[8,256]{1,0:T(8,128)} async-done(((f32[256,256]{1,0:T(8,128)}), f32[8,256]{1,0:T(8,128)}) %reduce-scatter.4.cloned.1.call-update) | async-done | bytes 8208 | tf_op jit(solution)/shard_map/reduce_scatter | solution.py:84
  368.7 0.7 multiply_divide_fusion.1
  369.5 14.3 %all_to_all.10 = f32[32,8,256]{2,1,0:T(8,128)S(1)} all-to-all(f32[32,8,256]{2,1,0:T(8,128)S(1)} %stack.201), channel_id=1, replica_groups=mesh['visit'=32,'tile'=8] {'visit'}, dimensions={0} | all-to-all | bytes 524288 | tf_op jit(solution)/shard_map/all_to_all | solution.py:74
  383.8 3.4 collective-permute-start.4
  387.2 2.7 collective-permute-start.5
  389.9 3.2 collective-permute-done.5
  393.1 11.2 %fusion.8 = f32[286,31,256]{2,0,1:T(8,128)S(1)} fusion(f32[256,31,256]{0,2,1:T(8,128)} %copy.7, f32[15,256]{1,0:T(8,128)S(1)} %collective-permute-done.5, f32[256,256]{1,0:T(8,128)S(1)} %bitcast.449, f32[15,256]{1,0:T(8,128)S(1)} %collective-permute-done.4), kind=kOutput, calls=%fused_computation.9 | convolution fusion | flops 6972652544 | bytes 17498112 | tf_op jit(solution)/shard_map/dot_general | solution.py:40
  404.2 0.8 fusion.50
  405.1 5.4 collective-permute-start.6
  410.5 2.1 collective-permute-start.7
  412.6 9.5 %collective-permute-done.7 = f32[1,15,256]{2,1,0:T(8,128)S(1)} collective-permute-done((f32[1,15,256]{2,1,0:T(8,128)S(1)}, f32[1,15,256]{2,1,0:T(8,128)S(1)}, u32[]{:S(2)}, u32[]{:S(2)}) %collective-permute-start.7) | collective-permute-done | bytes 15392 | tf_op jit(solution)/shard_map/ppermute | solution.py:17
  422.1 8.9 %fusion.4 = f32[286,31,256]{2,0,1:T(8,128)S(1)} fusion(f32[256,31,256]{0,2,1:T(8,128)S(1)} %bitcast.445, f32[1,15,256]{2,1,0:T(8,128)S(1)} %collective-permute-done.7, f32[1,256,256]{2,1,0:T(8,128)S(1)} %fusion.50, f32[1,15,256]{2,1,0:T(8,128)S(1)} %collective-permute-done.6), kind=kOutput, calls=%fused_computation.5 | convolution fusion | flops 6972652544 | bytes 17498112 | tf_op jit(solution)/shard_map/dot_general | solution.py:40
  431.1 1.4 fusion.34
  432.5 0.0 reduce-scatter.8.cloned.1.call-update
  432.5 146.0 %reduce-scatter.8.cloned.1.call-done = f32[8,256]{1,0:T(8,128)} async-done(((f32[256,256]{1,0:T(8,128)}), f32[8,256]{1,0:T(8,128)}) %reduce-scatter.8.cloned.1.call-update) | async-done | bytes 8208 | tf_op jit(solution)/shard_map/reduce_scatter | solution.py:84
  578.5 1.3 multiply_divide_fusion
  (23 shorter events, 0.1 us)
Async XLA Ops:
  7.9 25.3 %all-to-all-start = ((f32[32,8,256]{2,1,0:T(8,128)}), f32[32,8,256]{2,1,0:T(8,128)S(1)}, u32[]{:S(2)}, u32[]{:S(2)}) async-start(f32[32,8,256]{2,1,0:T(8,128)} %stack.68), calls=%async_computation | async-start | bytes 524288 | tf_op jit(solution)/shard_map/all_to_all | solution.py:74
  16.9 207.6 %reduce-scatter.6.cloned.1.call-start = ((), (), s32[]{:S(2)}) async-start(), calls=%async_computation.6 | async-start | bytes 270336 | tf_op jit(solution)/shard_map/reduce_scatter | solution.py:70
  33.3 16.0 %collective-permute-start = (f32[15,256]{1,0:T(8,128)S(1)}, f32[15,256]{1,0:T(8,128)S(1)}, u32[]{:S(2)}, u32[]{:S(2)}) collective-permute-start(f32[15,256]{1,0:T(8,128)S(1)} %get-tuple-element.11), channel_id=1, source_target_pairs={{0,1},{1,2},{2,3},{3,4},{4,5},{5,6},{6,7},{8,9},{9,10},{10,11},{11... | collective-permute-start | bytes 46088 | tf_op jit(solution)/shard_map/ppermute | solution.py:16
  36.7 12.6 %collective-permute-start.1 = (f32[15,256]{1,0:T(8,128)S(1)}, f32[15,256]{1,0:T(8,128)S(1)}, u32[]{:S(2)}, u32[]{:S(2)}) collective-permute-start(f32[15,256]{1,0:T(8,128)S(1)} %get-tuple-element.12), channel_id=1, source_target_pairs={{1,0},{2,1},{3,2},{4,3},{5,4},{6,5},{7,6},{9,8},{10,9},{11,10},{12... | collective-permute-start | bytes 46088 | tf_op jit(solution)/shard_map/ppermute | solution.py:17
  49.3 11.3 %copy-start = (f32[1,256,256]{2,1,0:T(8,128)S(1)}, f32[1,256,256]{2,1,0:T(8,128)}, u32[]{:S(2)}) copy-start(f32[1,256,256]{2,1,0:T(8,128)} %param.4) | copy-start | bytes 786436
  61.4 17.1 %collective-permute-start.2 = (f32[1,15,256]{2,1,0:T(8,128)S(1)}, f32[1,15,256]{2,1,0:T(8,128)S(1)}, u32[]{:S(2)}, u32[]{:S(2)}) collective-permute-start(f32[1,15,256]{2,1,0:T(8,128)S(1)} %get-tuple-element.9), channel_id=1, source_target_pairs={{0,1},{1,2},{2,3},{3,4},{4,5},{5,6},{6,7},{8,9},{9,10},{10,11},{11... | collective-permute-start | bytes 46088 | tf_op jit(solution)/shard_map/ppermute | solution.py:16
  64.8 13.7 %collective-permute-start.3 = (f32[1,15,256]{2,1,0:T(8,128)S(1)}, f32[1,15,256]{2,1,0:T(8,128)S(1)}, u32[]{:S(2)}, u32[]{:S(2)}) collective-permute-start(f32[1,15,256]{2,1,0:T(8,128)S(1)} %get-tuple-element.10), channel_id=1, source_target_pairs={{1,0},{2,1},{3,2},{4,3},{5,4},{6,5},{7,6},{9,8},{10,9},{11,10},{12... | collective-permute-start | bytes 46088 | tf_op jit(solution)/shard_map/ppermute | solution.py:17
  68.4 300.3 %reduce-scatter.4.cloned.1.call-start = ((), (), s32[]{:S(2)}) async-start(), calls=%async_computation.5 | async-start | bytes 270336 | tf_op jit(solution)/shard_map/reduce_scatter | solution.py:84
  89.7 279.0 %copy-start.1 = (f32[8,256]{1,0:T(8,128)S(1)}, f32[8,256]{1,0:T(8,128)}, u32[]{:S(2)}) copy-start(f32[8,256]{1,0:T(8,128)} %param.5) | copy-start | bytes 24580
  91.2 487.4 %reduce-scatter.8.cloned.1.call-start = ((), (), s32[]{:S(2)}) async-start(), calls=%async_computation.7 | async-start | bytes 270336 | tf_op jit(solution)/shard_map/reduce_scatter | solution.py:84
  369.4 52.7 %slice-start = ((s8[8126464]{0:T(1024)(128)(4,1)}), s8[4194304]{0:T(1024)(128)(4,1)S(1)}, s32[]{:S(2)}) async-start(s8[8126464]{0:T(1024)(128)(4,1)} %bitcast.444), calls=%async_computation.8 | async-start | bytes 8388608
  383.8 6.1 %collective-permute-start.4 = (f32[15,256]{1,0:T(8,128)S(1)}, f32[15,256]{1,0:T(8,128)S(1)}, u32[]{:S(2)}, u32[]{:S(2)}) collective-permute-start(f32[15,256]{1,0:T(8,128)S(1)} %get-tuple-element.7), channel_id=1, source_target_pairs={{0,1},{1,2},{2,3},{3,4},{4,5},{5,6},{6,7},{8,9},{9,10},{10,11},{11... | collective-permute-start | bytes 46088 | tf_op jit(solution)/shard_map/ppermute | solution.py:16
  387.2 35.0 %slice-start.1 = ((s8[8126464]{0:T(1024)(128)(4,1)}), s8[3932160]{0:T(1024)(128)(4,1)S(1)}, s32[]{:S(2)}) async-start(s8[8126464]{0:T(1024)(128)(4,1)} %bitcast.444), calls=%async_computation.9 | async-start | bytes 7864320
  387.2 5.9 %collective-permute-start.5 = (f32[15,256]{1,0:T(8,128)S(1)}, f32[15,256]{1,0:T(8,128)S(1)}, u32[]{:S(2)}, u32[]{:S(2)}) collective-permute-start(f32[15,256]{1,0:T(8,128)S(1)} %get-tuple-element.8), channel_id=1, source_target_pairs={{1,0},{2,1},{3,2},{4,3},{5,4},{6,5},{7,6},{9,8},{10,9},{11,10},{12... | collective-permute-start | bytes 46088 | tf_op jit(solution)/shard_map/ppermute | solution.py:17
  405.1 7.6 %collective-permute-start.6 = (f32[1,15,256]{2,1,0:T(8,128)S(1)}, f32[1,15,256]{2,1,0:T(8,128)S(1)}, u32[]{:S(2)}, u32[]{:S(2)}) collective-permute-start(f32[1,15,256]{2,1,0:T(8,128)S(1)} %get-tuple-element.5), channel_id=1, source_target_pairs={{0,1},{1,2},{2,3},{3,4},{4,5},{5,6},{6,7},{8,9},{9,10},{10,11},{11... | collective-permute-start | bytes 46088 | tf_op jit(solution)/shard_map/ppermute | solution.py:16
  410.5 11.7 %collective-permute-start.7 = (f32[1,15,256]{2,1,0:T(8,128)S(1)}, f32[1,15,256]{2,1,0:T(8,128)S(1)}, u32[]{:S(2)}, u32[]{:S(2)}) collective-permute-start(f32[1,15,256]{2,1,0:T(8,128)S(1)} %get-tuple-element.6), channel_id=1, source_target_pairs={{1,0},{2,1},{3,2},{4,3},{5,4},{6,5},{7,6},{9,8},{10,9},{11,10},{12... | collective-permute-start | bytes 46088 | tf_op jit(solution)/shard_map/ppermute | solution.py:17
  431.1 147.5 %copy-start.2 = (f32[8,256]{1,0:T(8,128)S(1)}, f32[8,256]{1,0:T(8,128)}, u32[]{:S(2)}) copy-start(f32[8,256]{1,0:T(8,128)} %reduce-scatter.6.cloned.1.call-done) | copy-start | bytes 24580
Sparse Core Ops, SparseCore 0:
  68.5 155.8 reduce-scatter.5
  226.9 141.7 reduce-scatter.3
  432.7 145.8 reduce-scatter.7
